TPU v7x, 32 devices: a whole 2x2x4 slice. The times are simulated.
32 devices in a mesh: slab: 8 (over z, y), grp: 4 (over x, core).
Axes of the slice: x: 2, y: 2, z: 4, core: 2. Of those that a mesh axis runs over, the one named last changes fastest.
Arguments:
- potential: bfloat16 [64, 8, 1024], P('slab'), may hold values from -3 to 3
- coefficients: bfloat16 [128, 16, 8, 1024], P(('slab', 'grp')), may hold values from -1 to 1
- box_center: int32 [128], replicated, may hold values from 0 to 63, as said below
- box_extent: int32 [128], replicated, may hold values from 8 to 16
Outputs:
- margin: float32 [128, 80], P(('slab', 'grp'))
- hamiltonian: float32 [128, 80], P(('slab', 'grp'))
Inputs may be any that keep to these rules, and one draw needn't show every extreme that they name: `box_center`: function b's centre lies among the 8 planes of slab b // 16, that is from (8 * (b // 16)) on.
All inputs are finite; a program needn't handle non-finite values.
Results may differ from a plain program's by a relative error of at most 0.0003.
Values may be sent and summed in bfloat16 or wider, within the bound.
A program may use at most 64 MiB of HBM per device.

v0:
```python
import jax
import jax.numpy as jnp
from jax import lax
from jax.sharding import PartitionSpec as P

COMP = 8
CX = 32
CY = 32


def with_halo(value, sides, width):
    for axis, dim in sides:
        size, length = (lax.axis_size(axis), value.shape[dim])
        up = [(i, (i + 1) % size) for i in range(size)]
        down = [(j, i) for i, j in up]
        last = lax.slice_in_dim(value, length - width, length, axis=dim)
        initial = lax.slice_in_dim(value, 0, width, axis=dim)
        before = lax.ppermute(last, axis, up)
        after = lax.ppermute(initial, axis, down)
        value = jnp.concatenate([before, value, after], axis=dim)
    return value


def shifted(value, axis, steps):
    count = lax.axis_size(axis)
    pairs = [(source, (source + steps) % count) for source in range(count)]
    return lax.ppermute(value, axis, pairs)


def haar_signs():
    row_ids = jnp.arange(COMP, dtype=jnp.int32)[:, None]
    col_ids = jnp.arange(COMP, dtype=jnp.int32)[None, :]
    common = jnp.bitwise_and(row_ids, col_ids)
    parity = (common % 2 + common // 2 % 2 + common // 4 % 2) % 2
    return (1 - 2 * parity).astype(jnp.float32)


def laplace_plane():
    cells = jnp.arange(CX * CY, dtype=jnp.int32)
    first_x = (cells // CY)[:, None]
    second_x = (cells // CY)[None, :]
    first_y = (cells % CY)[:, None]
    second_y = (cells % CY)[None, :]
    step_x = jnp.abs(first_x - second_x)
    step_y = jnp.abs(first_y - second_y)
    beside = (step_x == 1) & (first_y == second_y) | (step_y == 1) & (first_x == second_x)
    same_cell = (first_x == second_x) & (first_y == second_y)
    return jnp.where(same_cell, 2.0, jnp.where(beside, -0.5, 0.0)).astype(jnp.bfloat16)


def apply_hamiltonian(orbital, pot_box, inside):
    cell_count = orbital.shape[3]
    plane_term = jnp.dot(
        orbital.reshape(-1, cell_count), laplace_plane(), preferred_element_type=jnp.float32
    ).reshape(orbital.shape)
    padded = jnp.pad(orbital, ((0, 0), (1, 1), (0, 0), (0, 0)))
    depth_term = orbital.astype(jnp.float32) - 0.5 * (
        padded[:, :-2].astype(jnp.float32) + padded[:, 2:].astype(jnp.float32)
    )
    haar_table = haar_signs()
    fine_values = jnp.einsum(
        "kc,npcx->npkx",
        haar_table.astype(jnp.bfloat16),
        orbital,
        preferred_element_type=jnp.float32,
    )
    potential_term = (
        jnp.einsum(
            "kc,npkx->npcx",
            haar_table,
            pot_box.astype(jnp.float32) * fine_values,
            precision=lax.Precision.HIGHEST,
        )
        / COMP
    )
    return jnp.where(inside, plane_term + depth_term + potential_term, 0.0).astype(jnp.bfloat16)


def place_planes(starts, frame_depth, tile_data):
    source = jnp.arange(tile_data.shape[1], dtype=jnp.int32)
    target = jnp.arange(frame_depth, dtype=jnp.int32)
    onehot = (starts[:, None, None] + source[None, None, :] == target[None, :, None]).astype(
        jnp.bfloat16
    )
    placed = jnp.einsum("nqp,npcx->nqcx", onehot, tile_data, preferred_element_type=jnp.float32)
    return placed.astype(jnp.bfloat16)


def into_band(block_rows, offset, members):
    return jnp.pad(block_rows, ((0, 0), (offset * members, (2 - offset) * members)))


def local(potential, coefficients, box_center, box_extent):
    slab_index = lax.axis_index("slab")
    group_index = lax.axis_index("grp")
    groups = lax.axis_size("grp")
    per_device = coefficients.shape[0]
    box_depth = coefficients.shape[1]
    slab_depth = potential.shape[0]
    rim_depth = box_depth // 2
    frame_depth = slab_depth + box_depth
    members = groups * per_device
    first_row = (slab_index * groups + group_index) * per_device
    centers = lax.dynamic_slice_in_dim(box_center, first_row, per_device)
    extents = lax.dynamic_slice_in_dim(box_extent, first_row, per_device)
    frame_starts = centers - slab_index * slab_depth - extents // 2 + rim_depth
    planes = jnp.arange(box_depth, dtype=jnp.int32)
    inside = (planes[None, :] < extents[:, None])[:, :, None, None]
    orbital = jnp.where(inside, coefficients, jnp.zeros((), jnp.bfloat16))
    pot_frame = with_halo(potential, (("slab", 0),), rim_depth)
    padded_pot = jnp.pad(pot_frame, ((0, box_depth), (0, 0), (0, 0)))

    def cut_box(start_at):
        return lax.dynamic_slice_in_dim(padded_pot, start_at, box_depth, 0)

    pot_box = jax.vmap(cut_box)(frame_starts)
    applied = apply_hamiltonian(orbital, pot_box, inside)
    frame_orbital = place_planes(frame_starts, frame_depth, orbital)
    frame_applied = place_planes(frame_starts, frame_depth, applied)
    got_orbital, got_applied = (
        lax.all_to_all(frame_orbital, "grp", split_axis=3, concat_axis=0, tiled=True),
        lax.all_to_all(frame_applied, "grp", split_axis=3, concat_axis=0, tiled=True),
    )
    middle_orbital = got_orbital[:, rim_depth : rim_depth + slab_depth]
    middle_applied = got_applied[:, rim_depth : rim_depth + slab_depth]
    lower_set = None
    upper_set = None
    for direction in (1, -1):
        if direction == 1:
            sent_orbital = got_orbital[:, rim_depth + slab_depth :]
            sent_applied = got_applied[:, rim_depth + slab_depth :]
        else:
            sent_orbital = got_orbital[:, :rim_depth]
            sent_applied = got_applied[:, :rim_depth]
        came_orbital, came_applied = shifted((sent_orbital, sent_applied), "slab", direction)
        placed_pair = (came_orbital, came_applied)
        if direction == 1:
            lower_set = placed_pair
        else:
            upper_set = placed_pair
    tile_orbital = jnp.concatenate([lower_set[0], middle_orbital, upper_set[0]], axis=0)
    tile_applied = jnp.concatenate([lower_set[1], middle_applied, upper_set[1]], axis=0)
    flat_orbital = tile_orbital.reshape(tile_orbital.shape[0], -1)
    flat_applied = tile_applied.reshape(tile_applied.shape[0], -1)
    contract = (((1,), (1,)), ((), ()))
    part_margin = lax.dot_general(
        flat_orbital, flat_orbital, contract, preferred_element_type=jnp.float32
    )
    part_ham = lax.dot_general(
        flat_applied, flat_orbital, contract, preferred_element_type=jnp.float32
    )
    total_margin = into_band(part_margin[members : 2 * members], 1, members)
    total_ham = into_band(part_ham[members : 2 * members], 1, members)
    for direction in (1, -1):
        if direction == 1:
            sent_margin = part_margin[2 * members :]
            sent_ham = part_ham[2 * members :]
        else:
            sent_margin = part_margin[:members]
            sent_ham = part_ham[:members]
        came_margin, came_ham = shifted((sent_margin, sent_ham), "slab", direction)
        offset = 0 if direction == 1 else 2
        total_margin = total_margin + into_band(came_margin, offset, members)
        total_ham = total_ham + into_band(came_ham, offset, members)
    margin, hamiltonian = (
        lax.psum_scatter(total_margin, "grp", scatter_dimension=0, tiled=True),
        lax.psum_scatter(total_ham, "grp", scatter_dimension=0, tiled=True),
    )
    return (margin, hamiltonian)


def solution(mesh):
    return jax.shard_map(
        local,
        mesh=mesh,
        in_specs=(P("slab", None, None), P(("slab", "grp"), None, None, None), P(), P()),
        out_specs=(P(("slab", "grp"), None), P(("slab", "grp"), None)),
        check_vma=False,
    )
```

profile of v0, /device:TPU:0, one launch (start us, length us, event | category | flops | bytes accessed | tf_op | source)
XLA Modules:
  0.0 191.3 jit_solution(1780533823639298639)
XLA Ops:
  0.6 3.0 %collective-permute-start.4 = (bf16[8,8,1024]{2,1,0:T(8,128)(2,1)}, bf16[8,8,1024]{2,1,0:T(8,128)(2,1)S(1)}, u32[]{:S(2)}, u32[]{:S(2)}) collective-permute-start(bf16[8,8,1024]{2,1,0:T(8,128)(2,1)} %param.4), channel_id=1, source_target_pairs={{0,4},{4,8},{8,12},{12,16},{16,20},{20,24},{24,28},{28,0},{1,5},{5... | collective-permute-start | bytes 393224 | tf_op jit(solution)/shard_map/ppermute | solution.py:18
  3.7 3.1 %collective-permute-start.5 = (bf16[8,8,1024]{2,1,0:T(8,128)(2,1)}, bf16[8,8,1024]{2,1,0:T(8,128)(2,1)S(1)}, u32[]{:S(2)}, u32[]{:S(2)}) collective-permute-start(bf16[8,8,1024]{2,1,0:T(8,128)(2,1)} %param.4), channel_id=1, source_target_pairs={{4,0},{8,4},{12,8},{16,12},{20,16},{24,20},{28,24},{0,28},{5,1},{9... | collective-permute-start | bytes 393224 | tf_op jit(solution)/shard_map/ppermute | solution.py:19
  10.0 12.2 %copy.11 = bf16[4,24,8,1024]{1,2,0,3:T(8,128)(2,1)} copy(bf16[4,24,8,1024]{3,1,2,0:T(8,128)(2,1)S(1)} %convolution_convert_fusion.1) | data formatting | bytes 3145728 | tf_op jit(solution)/shard_map/convert_element_type | solution.py:86
  22.2 13.3 %reshape.116 = bf16[4,2,98304]{2,1,0:T(2,128)(2,1)} reshape(bf16[1024,4,8,24]{3,2,1,0:T(8,128)(2,1)} %bitcast.55) | data formatting | bytes 3145728
  35.5 4.5 %all-to-all-start = ((bf16[4,2,98304]{2,1,0:T(2,128)(2,1)}), bf16[4,2,98304]{2,1,0:T(2,128)(2,1)}, u32[]{:S(2)}, u32[]{:S(2)}) async-start(bf16[4,2,98304]{2,1,0:T(2,128)(2,1)} %reshape.116), calls=%async_computation | async-start | bytes 3145728 | tf_op jit(solution)/shard_map/all_to_all | solution.py:121
  40.1 5.2 %fusion.2 = f32[4,16,8,1024]{3,2,1,0:T(8,128)} fusion(bf16[4,16,8,1024]{3,2,1,0:T(8,128)(2,1)S(1)} %broadcast_select_fusion, s32[1024]{0:T(1024)S(1)} %get-tuple-element.19, s32[1024]{0:T(1024)S(1)} %get-tuple-element.20), kind=kOutput, calls=%fused_computation.9 | convolution fusion | flops 1089470464 | bytes 3153920 | tf_op jit(solution)/shard_map/dot_general | solution.py:53
  47.1 2.7 %gather_fusion = bf16[4,16,8,1024]{3,2,1,0:T(8,128)(2,1)} fusion(bf16[40,8,1024]{2,1,0:T(8,128)(2,1)} %fusion.31, s32[4]{0:T(128)S(1)} %get-tuple-element.4), kind=kCustom, calls=%fused_computation | custom fusion | bytes 2097200 | tf_op jit(solution)/shard_map/vmap()/gather | solution.py:114
  49.7 4.4 %fusion.5 = bf16[4,16,8,1024]{3,2,1,0:T(8,128)(2,1)S(1)} fusion(f32[4,16,8,1024]{3,2,1,0:T(8,128)} %fusion.2, bf16[4,16,8,1024]{3,2,1,0:T(8,128)(2,1)S(1)} %broadcast_select_fusion, f32[4,16,1024,8]{2,3,1,0:T(8,128)S(1)} %fusion.59, bf16[4,16,8,1024]{3,2,1,0:T(8,128)(2,1)} %gather_fusion, pred[4,16]{1,0:T(4,128)(4,1)S(1)} %iota_compare_fusion.2), kind=kOutput, calls=%fused_computation.12 | convolution fusion | flops 57151744 | bytes 7340096 | tf_op jit(solution)/shard_map/kc,npkx->npcx/dot_general | solution.py:68
  55.1 12.2 %copy.14 = bf16[4,24,8,1024]{1,2,0,3:T(8,128)(2,1)} copy(bf16[4,24,8,1024]{3,1,2,0:T(8,128)(2,1)S(1)} %convolution_convert_fusion) | data formatting | bytes 3145728 | tf_op jit(solution)/shard_map/convert_element_type | solution.py:86
  67.4 13.3 %reshape.118 = bf16[4,2,98304]{2,1,0:T(2,128)(2,1)} reshape(bf16[1024,4,8,24]{3,2,1,0:T(8,128)(2,1)} %bitcast.56) | data formatting | bytes 3145728
  80.6 3.8 %all-to-all-start.1 = ((bf16[4,2,98304]{2,1,0:T(2,128)(2,1)}), bf16[4,2,98304]{2,1,0:T(2,128)(2,1)S(1)}, u32[]{:S(2)}, u32[]{:S(2)}) async-start(bf16[4,2,98304]{2,1,0:T(2,128)(2,1)} %reshape.118), calls=%async_computation.1 | async-start | bytes 3145728 | tf_op jit(solution)/shard_map/all_to_all | solution.py:122
  84.4 14.1 %reshape.117 = bf16[1024,4,8,24]{3,2,1,0:T(8,128)(2,1)} reshape(bf16[4,2,98304]{2,1,0:T(2,128)(2,1)} %all-to-all-done) | data formatting | bytes 3145728
  98.5 12.8 %copy.12 = bf16[4,24,8,4,256]{4,0,3,2,1:T(4,128)(2,1)} copy(bf16[4,24,8,4,256]{1,2,0,4,3:T(8,128)(2,1)} %bitcast.57) | data formatting | bytes 3145728 | tf_op jit(solution)/shard_map/all_to_all | solution.py:121
  111.2 2.4 %all_to_all.29 = bf16[16,24,8,256]{3,0,2,1:T(8,128)(2,1)S(1)} reshape(bf16[4,4,24,8,256]{4,1,0,3,2:T(4,128)(2,1)} %bitcast.59) | data formatting | bytes 3145728 | tf_op jit(solution)/shard_map/all_to_all | solution.py:121
  114.8 4.7 %collective-permute-start.1 = (bf16[16,8,8,256]{3,0,2,1:T(8,128)(2,1)}, bf16[16,8,8,256]{3,0,2,1:T(8,128)(2,1)}, u32[]{:S(2)}, u32[]{:S(2)}) collective-permute-start(bf16[16,8,8,256]{3,0,2,1:T(8,128)(2,1)} %get-tuple-element.11), channel_id=1, source_target_pairs={{0,28},{4,0},{8,4},{12,8},{16,12},{20,16},{24,20},{28,24},{1,29},{... | collective-permute-start | bytes 1572872 | tf_op jit(solution)/shard_map/ppermute | solution.py:27
  119.5 13.4 %reshape.119 = bf16[1024,4,8,24]{3,2,1,0:T(8,128)(2,1)} reshape(bf16[4,2,98304]{2,1,0:T(2,128)(2,1)S(1)} %all-to-all-done.1) | data formatting | bytes 3145728
  132.9 12.3 %copy.15 = bf16[4,24,8,4,256]{4,0,3,2,1:T(4,128)(2,1)S(1)} copy(bf16[4,24,8,4,256]{1,2,0,4,3:T(8,128)(2,1)} %bitcast.58) | data formatting | bytes 3145728 | tf_op jit(solution)/shard_map/all_to_all | solution.py:122
  146.7 4.7 %collective-permute-start.7 = (bf16[16,8,8,256]{3,0,2,1:T(8,128)(2,1)S(1)}, bf16[16,8,8,256]{3,0,2,1:T(8,128)(2,1)S(1)}, u32[]{:S(2)}, u32[]{:S(2)}) collective-permute-start(bf16[16,8,8,256]{3,0,2,1:T(8,128)(2,1)S(1)} %get-tuple-element.8), channel_id=1, source_target_pairs={{0,28},{4,0},{8,4},{12,8},{16,12},{20,16},{24,20},{28,24},{1,29},{... | collective-permute-start | bytes 1572872 | tf_op jit(solution)/shard_map/ppermute | solution.py:27
  152.7 2.1 %convolution_bitcast_fusion = f32[48,48]{1,0:T(8,128)S(1)} fusion(bf16[16,8,8,256]{3,0,2,1:T(8,128)(2,1)} %collective-permute-done.1, bf16[16,8,8,256]{3,0,2,1:T(8,128)(2,1)S(1)} %copy-done, bf16[16,8,8,256]{3,0,2,1:T(8,128)(2,1)} %collective-permute-done), kind=kOutput, calls=%fused_computation.38 | convolution fusion | flops 80216064 | bytes 1582080 | tf_op jit(solution)/shard_map/dot_general | solution.py:146
  154.8 4.7 %collective-permute-start.3 = (f32[16,48]{1,0:T(8,128)S(1)}, f32[16,48]{1,0:T(8,128)S(1)}, u32[]{:S(2)}, u32[]{:S(2)}) collective-permute-start(f32[16,48]{1,0:T(8,128)S(1)} %get-tuple-element.17), channel_id=1, source_target_pairs={{0,28},{4,0},{8,4},{12,8},{16,12},{20,16},{24,20},{28,24},{1,29},{... | collective-permute-start | bytes 9224 | tf_op jit(solution)/shard_map/ppermute | solution.py:27
  159.6 9.9 %collective-permute-done.6 = bf16[16,8,8,256]{3,0,2,1:T(8,128)(2,1)S(1)} collective-permute-done((bf16[16,8,8,256]{3,0,2,1:T(8,128)(2,1)}, bf16[16,8,8,256]{3,0,2,1:T(8,128)(2,1)S(1)}, u32[]{:S(2)}, u32[]{:S(2)}) %collective-permute-start.6) | collective-permute-done | bytes 524320 | tf_op jit(solution)/shard_map/ppermute | solution.py:27
  169.5 2.2 %collective-permute-done.7 = bf16[16,8,8,256]{3,0,2,1:T(8,128)(2,1)S(1)} collective-permute-done((bf16[16,8,8,256]{3,0,2,1:T(8,128)(2,1)S(1)}, bf16[16,8,8,256]{3,0,2,1:T(8,128)(2,1)S(1)}, u32[]{:S(2)}, u32[]{:S(2)}) %collective-permute-start.7) | collective-permute-done | bytes 524320 | tf_op jit(solution)/shard_map/ppermute | solution.py:27
  173.7 4.6 %collective-permute-start.9 = (f32[16,48]{1,0:T(8,128)S(1)}, f32[16,48]{1,0:T(8,128)S(1)}, u32[]{:S(2)}, u32[]{:S(2)}) collective-permute-start(f32[16,48]{1,0:T(8,128)S(1)} %get-tuple-element.14), channel_id=1, source_target_pairs={{0,28},{4,0},{8,4},{12,8},{16,12},{20,16},{24,20},{28,24},{1,29},{... | collective-permute-start | bytes 9224 | tf_op jit(solution)/shard_map/ppermute | solution.py:27
  180.0 10.1 %all-reduce.11 = (f32[16,80]{1,0:T(8,128)S(1)}, f32[16,80]{1,0:T(8,128)S(1)}) all-reduce(f32[16,80]{1,0:T(8,128)S(1)} %pad_add_fusion.1, f32[16,80]{1,0:T(8,128)S(1)} %pad_add_fusion), channel_id=2, replica_groups=mesh['slab'=8,'grp'=4] {'grp'}, use_global_device_ids=true, to_apply=%region_0.1.clone | all-reduce | flops 2560 | bytes 20480
  (41 shorter events, 14.1 us)
Async XLA Ops:
  0.6 45.1 %collective-permute-start.4 = (bf16[8,8,1024]{2,1,0:T(8,128)(2,1)}, bf16[8,8,1024]{2,1,0:T(8,128)(2,1)S(1)}, u32[]{:S(2)}, u32[]{:S(2)}) collective-permute-start(bf16[8,8,1024]{2,1,0:T(8,128)(2,1)} %param.4), channel_id=1, source_target_pairs={{0,4},{4,8},{8,12},{12,16},{16,20},{20,24},{24,28},{28,0},{1,5},{5... | collective-permute-start | bytes 393224 | tf_op jit(solution)/shard_map/ppermute | solution.py:18
  3.7 42.1 %collective-permute-start.5 = (bf16[8,8,1024]{2,1,0:T(8,128)(2,1)}, bf16[8,8,1024]{2,1,0:T(8,128)(2,1)S(1)}, u32[]{:S(2)}, u32[]{:S(2)}) collective-permute-start(bf16[8,8,1024]{2,1,0:T(8,128)(2,1)} %param.4), channel_id=1, source_target_pairs={{4,0},{8,4},{12,8},{16,12},{20,16},{24,20},{28,24},{0,28},{5,1},{9... | collective-permute-start | bytes 393224 | tf_op jit(solution)/shard_map/ppermute | solution.py:19
  35.5 45.1 %all-to-all-start = ((bf16[4,2,98304]{2,1,0:T(2,128)(2,1)}), bf16[4,2,98304]{2,1,0:T(2,128)(2,1)}, u32[]{:S(2)}, u32[]{:S(2)}) async-start(bf16[4,2,98304]{2,1,0:T(2,128)(2,1)} %reshape.116), calls=%async_computation | async-start | bytes 3145728 | tf_op jit(solution)/shard_map/all_to_all | solution.py:121
  45.2 0.9 copy-start.1
  80.6 38.9 %all-to-all-start.1 = ((bf16[4,2,98304]{2,1,0:T(2,128)(2,1)}), bf16[4,2,98304]{2,1,0:T(2,128)(2,1)S(1)}, u32[]{:S(2)}, u32[]{:S(2)}) async-start(bf16[4,2,98304]{2,1,0:T(2,128)(2,1)} %reshape.118), calls=%async_computation.1 | async-start | bytes 3145728 | tf_op jit(solution)/shard_map/all_to_all | solution.py:122
  114.8 37.8 %collective-permute-start = (bf16[16,8,8,256]{3,0,2,1:T(8,128)(2,1)}, bf16[16,8,8,256]{3,0,2,1:T(8,128)(2,1)}, u32[]{:S(2)}, u32[]{:S(2)}) collective-permute-start(bf16[16,8,8,256]{3,0,2,1:T(8,128)(2,1)} %get-tuple-element.10), channel_id=1, source_target_pairs={{0,4},{4,8},{8,12},{12,16},{16,20},{20,24},{24,28},{28,0},{1,5},{5... | collective-permute-start | bytes 1572872 | tf_op jit(solution)/shard_map/ppermute | solution.py:27
  114.8 37.8 %collective-permute-start.1 = (bf16[16,8,8,256]{3,0,2,1:T(8,128)(2,1)}, bf16[16,8,8,256]{3,0,2,1:T(8,128)(2,1)}, u32[]{:S(2)}, u32[]{:S(2)}) collective-permute-start(bf16[16,8,8,256]{3,0,2,1:T(8,128)(2,1)} %get-tuple-element.11), channel_id=1, source_target_pairs={{0,28},{4,0},{8,4},{12,8},{16,12},{20,16},{24,20},{28,24},{1,29},{... | collective-permute-start | bytes 1572872 | tf_op jit(solution)/shard_map/ppermute | solution.py:27
  145.7 5.7 %copy-start.2 = (u32[32]{0:T(128)S(1)}, u32[32]{0:T(128)}, u32[]{:S(2)}) copy-start(u32[32]{0:T(128)} %constant.181) | copy-start | bytes 388
  145.7 6.9 %copy-start = (bf16[16,8,8,256]{3,0,2,1:T(8,128)(2,1)S(1)}, bf16[16,8,8,256]{3,0,2,1:T(8,128)(2,1)}, u32[]{:S(2)}) copy-start(bf16[16,8,8,256]{3,0,2,1:T(8,128)(2,1)} %get-tuple-element.12) | copy-start | bytes 1572868
  146.7 22.8 %collective-permute-start.6 = (bf16[16,8,8,256]{3,0,2,1:T(8,128)(2,1)}, bf16[16,8,8,256]{3,0,2,1:T(8,128)(2,1)S(1)}, u32[]{:S(2)}, u32[]{:S(2)}) collective-permute-start(bf16[16,8,8,256]{3,0,2,1:T(8,128)(2,1)} %get-tuple-element.7), channel_id=1, source_target_pairs={{0,4},{4,8},{8,12},{12,16},{16,20},{20,24},{24,28},{28,0},{1,5},{5... | collective-permute-start | bytes 1572872 | tf_op jit(solution)/shard_map/ppermute | solution.py:27
  146.7 25.0 %collective-permute-start.7 = (bf16[16,8,8,256]{3,0,2,1:T(8,128)(2,1)S(1)}, bf16[16,8,8,256]{3,0,2,1:T(8,128)(2,1)S(1)}, u32[]{:S(2)}, u32[]{:S(2)}) collective-permute-start(bf16[16,8,8,256]{3,0,2,1:T(8,128)(2,1)S(1)} %get-tuple-element.8), channel_id=1, source_target_pairs={{0,28},{4,0},{8,4},{12,8},{16,12},{20,16},{24,20},{28,24},{1,29},{... | collective-permute-start | bytes 1572872 | tf_op jit(solution)/shard_map/ppermute | solution.py:27
  154.8 23.5 %collective-permute-start.2 = (f32[16,48]{1,0:T(8,128)S(1)}, f32[16,48]{1,0:T(8,128)S(1)}, u32[]{:S(2)}, u32[]{:S(2)}) collective-permute-start(f32[16,48]{1,0:T(8,128)S(1)} %get-tuple-element.18), channel_id=1, source_target_pairs={{0,4},{4,8},{8,12},{12,16},{16,20},{20,24},{24,28},{28,0},{1,5},{5... | collective-permute-start | bytes 9224 | tf_op jit(solution)/shard_map/ppermute | solution.py:27
  154.8 23.4 %collective-permute-start.3 = (f32[16,48]{1,0:T(8,128)S(1)}, f32[16,48]{1,0:T(8,128)S(1)}, u32[]{:S(2)}, u32[]{:S(2)}) collective-permute-start(f32[16,48]{1,0:T(8,128)S(1)} %get-tuple-element.17), channel_id=1, source_target_pairs={{0,28},{4,0},{8,4},{12,8},{16,12},{20,16},{24,20},{28,24},{1,29},{... | collective-permute-start | bytes 9224 | tf_op jit(solution)/shard_map/ppermute | solution.py:27
  173.5 6.4 %collective-permute-start.8 = (f32[16,48]{1,0:T(8,128)S(1)}, f32[16,48]{1,0:T(8,128)S(1)}, u32[]{:S(2)}, u32[]{:S(2)}) collective-permute-start(f32[16,48]{1,0:T(8,128)S(1)} %get-tuple-element.15), channel_id=1, source_target_pairs={{0,4},{4,8},{8,12},{12,16},{16,20},{20,24},{24,28},{28,0},{1,5},{5... | collective-permute-start | bytes 9224 | tf_op jit(solution)/shard_map/ppermute | solution.py:27
  173.7 6.2 %collective-permute-start.9 = (f32[16,48]{1,0:T(8,128)S(1)}, f32[16,48]{1,0:T(8,128)S(1)}, u32[]{:S(2)}, u32[]{:S(2)}) collective-permute-start(f32[16,48]{1,0:T(8,128)S(1)} %get-tuple-element.14), channel_id=1, source_target_pairs={{0,28},{4,0},{8,4},{12,8},{16,12},{20,16},{24,20},{28,24},{1,29},{... | collective-permute-start | bytes 9224 | tf_op jit(solution)/shard_map/ppermute | solution.py:27
where the time goes:
time: 192 us; the launch traced here: 191 us
  local copies, waits for them, and re-layouts  113 us (59%)
  starting transfers between devices  33.5 us (17%)
  matrix products  15.8 us (8%)
  waiting for transfers between devices  13.7 us (7%)
  blocking collectives  10.1 us (5%)
  other arithmetic  3.34 us (2%)
    unnamed x13, local copies, waits for them, and re-layouts  56.2 us
    convert_element_type x2, local copies, waits for them, and re-layouts, place_planes(): return placed.astype(jnp.bfloat16)  24.4 us
    ppermute x8, starting transfers between devices, shifted(): return lax.ppermute(value, axis, pairs)  19 us
    all_to_all x2, local copies, waits for them, and re-layouts, local(): lax.all_to_all(frame_orbital, 'grp', split_axis=3, concat_axis=0, tiled=T...  15.1 us
    ppermute x8, waiting for transfers between devices, shifted(): return lax.ppermute(value, axis, pairs)  13.7 us
    all_to_all x2, local copies, waits for them, and re-layouts, local(): lax.all_to_all(frame_applied, 'grp', split_axis=3, concat_axis=0, tiled=T...  12.8 us
    unnamed x1, blocking collectives  10.1 us
    dot_general x1, matrix products, apply_hamiltonian(): jnp.dot(orbital.reshape(-1, cell_count), laplace_plane(), preferred_eleme...  5.15 us
  transfers between devices with their start and end apart: 12, of which 3 were waited for; matrix products, arithmetic and copies ran while one was open for 67% of the time, Pallas kernels for 0%

commit v1 on v0

--- a/solution.py
+++ b/solution.py
@@ -119,7 +119,12 @@
     frame_applied = place_planes(frame_starts, frame_depth, applied)
     got_orbital, got_applied = (
         lax.all_to_all(frame_orbital, "grp", split_axis=3, concat_axis=0, tiled=True),
-        lax.all_to_all(frame_applied, "grp", split_axis=3, concat_axis=0, tiled=True),
+        jnp.concatenate(
+            lax.all_to_all(
+                jnp.stack(jnp.split(frame_applied, lax.axis_size("grp"), axis=3)), "grp", 0, 0
+            ),
+            axis=0,
+        ),
     )
     middle_orbital = got_orbital[:, rim_depth : rim_depth + slab_depth]
     middle_applied = got_applied[:, rim_depth : rim_depth + slab_depth]

time: 192 us -> 168 us (0.88)
  local copies, waits for them, and re-layouts: 113 us -> 62 us
  waiting for transfers between devices: 13.7 us -> 39.4 us
    unnamed x13 -> x14, local copies, waits for them, and re-layouts: 56.2 us -> 30.4 us
    ppermute x8, waiting for transfers between devices: 13.7 us -> 36.2 us  [shifted(): return lax.ppermute(value, axis, pairs)]
    all_to_all x2 -> x0, local copies, waits for them, and re-layouts: 12.8 us -> none  [local(): lax.all_to_all(frame_applied, 'grp', split_axis=3, concat_axis=0, tiled=T...]
    convert_element_type x2 -> x1, local copies, waits for them, and re-layouts: 24.4 us -> 12.2 us  [place_planes(): return placed.astype(jnp.bfloat16)]
    all_to_all x1, waiting for transfers between devices: 0.01 us -> 3.28 us  [local(): lax.all_to_all(frame_orbital, 'grp', split_axis=3, concat_axis=0, tiled=T...]
    ppermute x1, starting transfers between devices: 3.05 us -> 0.01 us  [with_halo(): before = lax.ppermute(last, axis, up)]
    ppermute x1, starting transfers between devices: 3.11 us -> 6.09 us  [with_halo(): after = lax.ppermute(initial, axis, down)]
  transfers between devices with their start and end apart: 12 -> 12, of which waited for: 3 -> 5; matrix products, arithmetic and copies ran while one was open for 67% -> 47% of each run, Pallas kernels for 0% -> 0%
where the time goes in v1:
time: 168 us; the launch traced here: 167 us
  local copies, waits for them, and re-layouts  62 us (37%)
  waiting for transfers between devices  39.4 us (23%)
  starting transfers between devices  33.6 us (20%)
  matrix products  15.6 us (9%)
  blocking collectives  10.1 us (6%)
  other arithmetic  4.75 us (3%)
    ppermute x8, waiting for transfers between devices, shifted(): return lax.ppermute(value, axis, pairs)  36.2 us
    unnamed x14, local copies, waits for them, and re-layouts  30.4 us
    ppermute x8, starting transfers between devices, shifted(): return lax.ppermute(value, axis, pairs)  19.4 us
    all_to_all x2, local copies, waits for them, and re-layouts, local(): lax.all_to_all(frame_orbital, 'grp', split_axis=3, concat_axis=0, tiled=T...  15.1 us
    convert_element_type x1, local copies, waits for them, and re-layouts, place_planes(): return placed.astype(jnp.bfloat16)  12.2 us
    unnamed x1, blocking collectives  10.1 us
    ppermute x1, starting transfers between devices, with_halo(): after = lax.ppermute(initial, axis, down)  6.09 us
    dot_general x1, matrix products, apply_hamiltonian(): jnp.dot(orbital.reshape(-1, cell_count), laplace_plane(), preferred_eleme...  5.15 us
  transfers between devices with their start and end apart: 12, of which 5 were waited for; matrix products, arithmetic and copies ran while one was open for 47% of the time, Pallas kernels for 0%

profile of v1, /device:TPU:0, one launch (start us, length us, event | category | flops | bytes accessed | tf_op | source)
XLA Modules:
  0.0 166.9 jit_solution(11768307259067228092)
XLA Ops:
  0.6 6.1 %collective-permute-start.5 = (bf16[8,8,1024]{2,1,0:T(8,128)(2,1)}, bf16[8,8,1024]{2,1,0:T(8,128)(2,1)S(1)}, u32[]{:S(2)}, u32[]{:S(2)}) collective-permute-start(bf16[8,8,1024]{2,1,0:T(8,128)(2,1)} %param.4), channel_id=1, source_target_pairs={{4,0},{8,4},{12,8},{16,12},{20,16},{24,20},{28,24},{0,28},{5,1},{9... | collective-permute-start | bytes 393224 | tf_op jit(solution)/shard_map/ppermute | solution.py:19
  7.6 1.4 broadcast_select_fusion
  10.0 12.2 %copy.13 = bf16[4,24,8,1024]{1,2,0,3:T(8,128)(2,1)} copy(bf16[4,24,8,1024]{3,1,2,0:T(8,128)(2,1)S(1)} %convolution_convert_fusion.1) | data formatting | bytes 3145728 | tf_op jit(solution)/shard_map/convert_element_type | solution.py:86
  22.2 13.3 %reshape.120 = bf16[4,2,98304]{2,1,0:T(2,128)(2,1)} reshape(bf16[1024,4,8,24]{3,2,1,0:T(8,128)(2,1)} %bitcast.58) | data formatting | bytes 3145728
  35.5 4.5 %all-to-all-start = ((bf16[4,2,98304]{2,1,0:T(2,128)(2,1)}), bf16[4,2,98304]{2,1,0:T(2,128)(2,1)}, u32[]{:S(2)}, u32[]{:S(2)}) async-start(bf16[4,2,98304]{2,1,0:T(2,128)(2,1)} %reshape.120), calls=%async_computation | async-start | bytes 3145728 | tf_op jit(solution)/shard_map/all_to_all | solution.py:121
  40.0 5.2 %fusion.2 = f32[4,16,8,1024]{3,2,1,0:T(8,128)} fusion(bf16[4,16,8,1024]{3,2,1,0:T(8,128)(2,1)S(1)} %broadcast_select_fusion, s32[1024]{0:T(1024)S(1)} %get-tuple-element.23, s32[1024]{0:T(1024)S(1)} %get-tuple-element.24), kind=kOutput, calls=%fused_computation.9 | convolution fusion | flops 1089470464 | bytes 3153920 | tf_op jit(solution)/shard_map/dot_general | solution.py:53
  47.0 2.7 %gather_fusion = bf16[4,16,8,1024]{3,2,1,0:T(8,128)(2,1)} fusion(bf16[40,8,1024]{2,1,0:T(8,128)(2,1)} %fusion.31, s32[4]{0:T(128)S(1)} %get-tuple-element.4), kind=kCustom, calls=%fused_computation | custom fusion | bytes 2097200 | tf_op jit(solution)/shard_map/vmap()/gather | solution.py:114
  49.7 4.4 %fusion.5 = bf16[4,16,8,1024]{3,2,1,0:T(8,128)(2,1)S(1)} fusion(f32[4,16,8,1024]{3,2,1,0:T(8,128)} %fusion.2, bf16[4,16,8,1024]{3,2,1,0:T(8,128)(2,1)S(1)} %broadcast_select_fusion, f32[4,16,1024,8]{2,3,1,0:T(8,128)S(1)} %fusion.59, bf16[4,16,8,1024]{3,2,1,0:T(8,128)(2,1)} %gather_fusion, pred[4,16]{1,0:T(4,128)(4,1)S(1)} %iota_compare_fusion.2), kind=kOutput, calls=%fused_computation.12 | convolution fusion | flops 57151744 | bytes 7340096 | tf_op jit(solution)/shard_map/kc,npkx->npcx/dot_general | solution.py:68
  55.3 1.4 pad_maximum_fusion.1
  56.7 3.3 %all-to-all-done = bf16[4,2,98304]{2,1,0:T(2,128)(2,1)} async-done(((bf16[4,2,98304]{2,1,0:T(2,128)(2,1)}), bf16[4,2,98304]{2,1,0:T(2,128)(2,1)}, u32[]{:S(2)}, u32[]{:S(2)}) %all-to-all-start) | async-done | bytes 1572896 | tf_op jit(solution)/shard_map/all_to_all | solution.py:121
  60.0 3.6 %all-to-all-start.1 = ((bf16[4,4,24,8,256]{4,2,3,1,0:T(8,128)(2,1)}), bf16[4,4,24,8,256]{4,2,3,1,0:T(8,128)(2,1)S(1)}, u32[]{:S(2)}, u32[]{:S(2)}) async-start(bf16[4,4,24,8,256]{4,2,3,1,0:T(8,128)(2,1)} %pad_maximum_fusion.1), calls=%async_computation.1 | async-start | bytes 3145728 | tf_op jit(solution)/shard_map/all_to_all | solution.py:123
  63.5 14.1 %reshape.121 = bf16[1024,4,8,24]{3,2,1,0:T(8,128)(2,1)} reshape(bf16[4,2,98304]{2,1,0:T(2,128)(2,1)} %all-to-all-done) | data formatting | bytes 3145728
  77.6 12.8 %copy.14 = bf16[4,24,8,4,256]{4,0,3,2,1:T(4,128)(2,1)} copy(bf16[4,24,8,4,256]{1,2,0,4,3:T(8,128)(2,1)} %bitcast.59) | data formatting | bytes 3145728 | tf_op jit(solution)/shard_map/all_to_all | solution.py:121
  90.4 2.4 %all_to_all.19 = bf16[16,24,8,256]{3,0,2,1:T(8,128)(2,1)S(1)} reshape(bf16[4,4,24,8,256]{4,1,0,3,2:T(4,128)(2,1)} %bitcast.61) | data formatting | bytes 3145728 | tf_op jit(solution)/shard_map/all_to_all | solution.py:121
  93.9 4.7 %collective-permute-start.1 = (bf16[16,8,8,256]{3,0,2,1:T(8,128)(2,1)}, bf16[16,8,8,256]{3,0,2,1:T(8,128)(2,1)S(1)}, u32[]{:S(2)}, u32[]{:S(2)}) collective-permute-start(bf16[16,8,8,256]{3,0,2,1:T(8,128)(2,1)} %get-tuple-element.15), channel_id=1, source_target_pairs={{0,28},{4,0},{8,4},{12,8},{16,12},{20,16},{24,20},{28,24},{1,29},{... | collective-permute-start | bytes 1572872 | tf_op jit(solution)/shard_map/ppermute | solution.py:27
  99.1 4.8 %collective-permute-start.7 = (bf16[16,8,8,256]{3,0,2,1:T(8,128)(2,1)S(1)}, bf16[16,8,8,256]{3,0,2,1:T(8,128)(2,1)}, u32[]{:S(2)}, u32[]{:S(2)}) collective-permute-start(bf16[16,8,8,256]{3,0,2,1:T(8,128)(2,1)S(1)} %copy.27), channel_id=1, source_target_pairs={{0,28},{4,0},{8,4},{12,8},{16,12},{20,16},{24,20},{28,24},{1,29},{... | collective-permute-start | bytes 1572872 | tf_op jit(solution)/shard_map/ppermute | solution.py:27
  105.8 25.6 %collective-permute-done.1 = bf16[16,8,8,256]{3,0,2,1:T(8,128)(2,1)S(1)} collective-permute-done((bf16[16,8,8,256]{3,0,2,1:T(8,128)(2,1)}, bf16[16,8,8,256]{3,0,2,1:T(8,128)(2,1)S(1)}, u32[]{:S(2)}, u32[]{:S(2)}) %collective-permute-start.1) | collective-permute-done | bytes 524320 | tf_op jit(solution)/shard_map/ppermute | solution.py:27
  131.4 1.7 %convolution_bitcast_fusion = f32[48,48]{1,0:T(8,128)S(1)} fusion(bf16[16,8,8,256]{3,0,2,1:T(8,128)(2,1)S(1)} %collective-permute-done.1, bf16[16,8,8,256]{3,0,2,1:T(8,128)(2,1)S(1)} %copy-done, bf16[16,8,8,256]{3,0,2,1:T(8,128)(2,1)} %collective-permute-done), kind=kOutput, calls=%fused_computation.39 | convolution fusion | flops 80216064 | bytes 1582080 | tf_op jit(solution)/shard_map/dot_general | solution.py:151
  133.2 4.9 %collective-permute-start.3 = (f32[16,48]{1,0:T(8,128)S(1)}, f32[16,48]{1,0:T(8,128)S(1)}, u32[]{:S(2)}, u32[]{:S(2)}) collective-permute-start(f32[16,48]{1,0:T(8,128)S(1)} %get-tuple-element.21), channel_id=1, source_target_pairs={{0,28},{4,0},{8,4},{12,8},{16,12},{20,16},{24,20},{28,24},{1,29},{... | collective-permute-start | bytes 9224 | tf_op jit(solution)/shard_map/ppermute | solution.py:27
  138.1 4.3 %collective-permute-done.7 = bf16[16,8,8,256]{3,0,2,1:T(8,128)(2,1)} collective-permute-done((bf16[16,8,8,256]{3,0,2,1:T(8,128)(2,1)S(1)}, bf16[16,8,8,256]{3,0,2,1:T(8,128)(2,1)}, u32[]{:S(2)}, u32[]{:S(2)}) %collective-permute-start.7) | collective-permute-done | bytes 524320 | tf_op jit(solution)/shard_map/ppermute | solution.py:27
  142.4 1.9 %fusion.25 = f32[48,48]{1,0:T(8,128)S(1)} fusion(bf16[16,8,8,256]{3,0,2,1:T(8,128)(2,1)} %collective-permute-done.7, bf16[16,8,8,256]{3,0,2,1:T(8,128)(2,1)S(1)} %copy.26, bf16[16,8,8,256]{3,0,2,1:T(8,128)(2,1)} %collective-permute-done.6, bf16[16,8,8,256]{3,0,2,1:T(8,128)(2,1)S(1)} %collective-permute-done.1, bf16[16,8,8,256]{3,0,2,1:T(8,128)(2,1)S(1)} %copy-done, ...), kind=kOutput, calls=%fused_computation.38 | convolution fusion | flops 84934656 | bytes 3154944 | tf_op jit(solution)/shard_map/dot_general | solution.py:154
  144.3 4.9 %collective-permute-start.9 = (f32[16,48]{1,0:T(8,128)S(1)}, f32[16,48]{1,0:T(8,128)S(1)}, u32[]{:S(2)}, u32[]{:S(2)}) collective-permute-start(f32[16,48]{1,0:T(8,128)S(1)} %get-tuple-element.18), channel_id=1, source_target_pairs={{0,28},{4,0},{8,4},{12,8},{16,12},{20,16},{24,20},{28,24},{1,29},{... | collective-permute-start | bytes 9224 | tf_op jit(solution)/shard_map/ppermute | solution.py:27
  150.6 5.0 %collective-permute-done.8 = f32[16,48]{1,0:T(8,128)S(1)} collective-permute-done((f32[16,48]{1,0:T(8,128)S(1)}, f32[16,48]{1,0:T(8,128)S(1)}, u32[]{:S(2)}, u32[]{:S(2)}) %collective-permute-start.8) | collective-permute-done | bytes 3104 | tf_op jit(solution)/shard_map/ppermute | solution.py:27
  155.6 10.1 %all-reduce.11 = (f32[16,80]{1,0:T(8,128)S(1)}, f32[16,80]{1,0:T(8,128)S(1)}) all-reduce(f32[16,80]{1,0:T(8,128)S(1)} %pad_add_fusion.1, f32[16,80]{1,0:T(8,128)S(1)} %pad_add_fusion), channel_id=2, replica_groups=mesh['slab'=8,'grp'=4] {'grp'}, use_global_device_ids=true, to_apply=%region_0.1.clone | all-reduce | flops 2560 | bytes 20480
  (41 shorter events, 10.3 us)
Async XLA Ops:
  0.6 45.0 %collective-permute-start.5 = (bf16[8,8,1024]{2,1,0:T(8,128)(2,1)}, bf16[8,8,1024]{2,1,0:T(8,128)(2,1)S(1)}, u32[]{:S(2)}, u32[]{:S(2)}) collective-permute-start(bf16[8,8,1024]{2,1,0:T(8,128)(2,1)} %param.4), channel_id=1, source_target_pairs={{4,0},{8,4},{12,8},{16,12},{20,16},{24,20},{28,24},{0,28},{5,1},{9... | collective-permute-start | bytes 393224 | tf_op jit(solution)/shard_map/ppermute | solution.py:19
  6.7 39.0 %collective-permute-start.4 = (bf16[8,8,1024]{2,1,0:T(8,128)(2,1)}, bf16[8,8,1024]{2,1,0:T(8,128)(2,1)S(1)}, u32[]{:S(2)}, u32[]{:S(2)}) collective-permute-start(bf16[8,8,1024]{2,1,0:T(8,128)(2,1)} %param.4), channel_id=1, source_target_pairs={{0,4},{4,8},{8,12},{12,16},{16,20},{20,24},{24,28},{28,0},{1,5},{5... | collective-permute-start | bytes 393224 | tf_op jit(solution)/shard_map/ppermute | solution.py:18
  35.5 24.5 %all-to-all-start = ((bf16[4,2,98304]{2,1,0:T(2,128)(2,1)}), bf16[4,2,98304]{2,1,0:T(2,128)(2,1)}, u32[]{:S(2)}, u32[]{:S(2)}) async-start(bf16[4,2,98304]{2,1,0:T(2,128)(2,1)} %reshape.120), calls=%async_computation | async-start | bytes 3145728 | tf_op jit(solution)/shard_map/all_to_all | solution.py:121
  45.2 0.9 copy-start.1
  60.0 38.7 %all-to-all-start.1 = ((bf16[4,4,24,8,256]{4,2,3,1,0:T(8,128)(2,1)}), bf16[4,4,24,8,256]{4,2,3,1,0:T(8,128)(2,1)S(1)}, u32[]{:S(2)}, u32[]{:S(2)}) async-start(bf16[4,4,24,8,256]{4,2,3,1,0:T(8,128)(2,1)} %pad_maximum_fusion.1), calls=%async_computation.1 | async-start | bytes 3145728 | tf_op jit(solution)/shard_map/all_to_all | solution.py:123
  93.9 37.5 %collective-permute-start.1 = (bf16[16,8,8,256]{3,0,2,1:T(8,128)(2,1)}, bf16[16,8,8,256]{3,0,2,1:T(8,128)(2,1)S(1)}, u32[]{:S(2)}, u32[]{:S(2)}) collective-permute-start(bf16[16,8,8,256]{3,0,2,1:T(8,128)(2,1)} %get-tuple-element.15), channel_id=1, source_target_pairs={{0,28},{4,0},{8,4},{12,8},{16,12},{20,16},{24,20},{28,24},{1,29},{... | collective-permute-start | bytes 1572872 | tf_op jit(solution)/shard_map/ppermute | solution.py:27
  98.7 32.8 %collective-permute-start = (bf16[16,8,8,256]{3,0,2,1:T(8,128)(2,1)}, bf16[16,8,8,256]{3,0,2,1:T(8,128)(2,1)}, u32[]{:S(2)}, u32[]{:S(2)}) collective-permute-start(bf16[16,8,8,256]{3,0,2,1:T(8,128)(2,1)} %get-tuple-element.14), channel_id=1, source_target_pairs={{0,4},{4,8},{8,12},{12,16},{16,20},{20,24},{24,28},{28,0},{1,5},{5... | collective-permute-start | bytes 1572872 | tf_op jit(solution)/shard_map/ppermute | solution.py:27
  98.7 5.6 %copy-start.2 = (u32[32]{0:T(128)S(1)}, u32[32]{0:T(128)}, u32[]{:S(2)}) copy-start(u32[32]{0:T(128)} %constant.181) | copy-start | bytes 388
  98.8 32.6 %copy-start = (bf16[16,8,8,256]{3,0,2,1:T(8,128)(2,1)S(1)}, bf16[16,8,8,256]{3,0,2,1:T(8,128)(2,1)}, u32[]{:S(2)}) copy-start(bf16[16,8,8,256]{3,0,2,1:T(8,128)(2,1)} %get-tuple-element.16) | copy-start | bytes 1572868
  99.1 43.2 %collective-permute-start.7 = (bf16[16,8,8,256]{3,0,2,1:T(8,128)(2,1)S(1)}, bf16[16,8,8,256]{3,0,2,1:T(8,128)(2,1)}, u32[]{:S(2)}, u32[]{:S(2)}) collective-permute-start(bf16[16,8,8,256]{3,0,2,1:T(8,128)(2,1)S(1)} %copy.27), channel_id=1, source_target_pairs={{0,28},{4,0},{8,4},{12,8},{16,12},{20,16},{24,20},{28,24},{1,29},{... | collective-permute-start | bytes 1572872 | tf_op jit(solution)/shard_map/ppermute | solution.py:27
  104.2 38.2 %collective-permute-start.6 = (bf16[16,8,8,256]{3,0,2,1:T(8,128)(2,1)S(1)}, bf16[16,8,8,256]{3,0,2,1:T(8,128)(2,1)}, u32[]{:S(2)}, u32[]{:S(2)}) collective-permute-start(bf16[16,8,8,256]{3,0,2,1:T(8,128)(2,1)S(1)} %copy.25), channel_id=1, source_target_pairs={{0,4},{4,8},{8,12},{12,16},{16,20},{20,24},{24,28},{28,0},{1,5},{5... | collective-permute-start | bytes 1572872 | tf_op jit(solution)/shard_map/ppermute | solution.py:27
  133.2 16.0 %collective-permute-start.3 = (f32[16,48]{1,0:T(8,128)S(1)}, f32[16,48]{1,0:T(8,128)S(1)}, u32[]{:S(2)}, u32[]{:S(2)}) collective-permute-start(f32[16,48]{1,0:T(8,128)S(1)} %get-tuple-element.21), channel_id=1, source_target_pairs={{0,28},{4,0},{8,4},{12,8},{16,12},{20,16},{24,20},{28,24},{1,29},{... | collective-permute-start | bytes 9224 | tf_op jit(solution)/shard_map/ppermute | solution.py:27
  138.1 11.2 %collective-permute-start.2 = (f32[16,48]{1,0:T(8,128)S(1)}, f32[16,48]{1,0:T(8,128)S(1)}, u32[]{:S(2)}, u32[]{:S(2)}) collective-permute-start(f32[16,48]{1,0:T(8,128)S(1)} %get-tuple-element.22), channel_id=1, source_target_pairs={{0,4},{4,8},{8,12},{12,16},{16,20},{20,24},{24,28},{28,0},{1,5},{5... | collective-permute-start | bytes 9224 | tf_op jit(solution)/shard_map/ppermute | solution.py:27
  144.3 6.3 %collective-permute-start.9 = (f32[16,48]{1,0:T(8,128)S(1)}, f32[16,48]{1,0:T(8,128)S(1)}, u32[]{:S(2)}, u32[]{:S(2)}) collective-permute-start(f32[16,48]{1,0:T(8,128)S(1)} %get-tuple-element.18), channel_id=1, source_target_pairs={{0,28},{4,0},{8,4},{12,8},{16,12},{20,16},{24,20},{28,24},{1,29},{... | collective-permute-start | bytes 9224 | tf_op jit(solution)/shard_map/ppermute | solution.py:27
  149.2 6.3 %collective-permute-start.8 = (f32[16,48]{1,0:T(8,128)S(1)}, f32[16,48]{1,0:T(8,128)S(1)}, u32[]{:S(2)}, u32[]{:S(2)}) collective-permute-start(f32[16,48]{1,0:T(8,128)S(1)} %get-tuple-element.19), channel_id=1, source_target_pairs={{0,4},{4,8},{8,12},{12,16},{16,20},{20,24},{24,28},{28,0},{1,5},{5... | collective-permute-start | bytes 9224 | tf_op jit(solution)/shard_map/ppermute | solution.py:27
